TPU v7x, 128 devices: a whole 4x4x4 slice. The times are simulated.
128 devices in a mesh: dp: 32 (over z, y, core), mp: 4 (over x).
Axes of the slice: x: 4, y: 4, z: 4, core: 2. Of those that a mesh axis runs over, the one named last changes fastest.
Arguments:
- states: bfloat16 [128, 512, 1024], P('dp'), may hold values from -72 to 72
- lengths: int32 [128], P('dp'), may hold values from 64 to 512
- attn_in: bfloat16 [3, 1024, 1024], P(None, None, 'mp'), may hold values from -0.1875 to 0.1875
- attn_out: bfloat16 [1024, 1024], P('mp'), may hold values from -0.1875 to 0.1875
- attn_gain: float32 [1024], replicated, may hold values from 0.1 to 1.9
- ffn_up: bfloat16 [1024, 4096], P(None, 'mp'), may hold values from -0.1875 to 0.1875
- ffn_down: bfloat16 [4096, 1024], P('mp'), may hold values from -0.09375 to 0.09375
- ffn_gain: float32 [1024], replicated, may hold values from 0.1 to 1.9
- centroids: bfloat16 [65536, 1024], P(('dp', 'mp')), may hold values from -0.59765625 to 0.59765625
- assignment: int32 [128], replicated, may hold values from 0 to 65535
- list_place: int32 [65536], replicated, may hold values from 0 to 65535, as said below
Outputs:
- codes: float32 [128, 1024], P(('dp', 'mp'))
- lower: float32 [1024], replicated
- upper: float32 [1024], replicated
Inputs may be any that keep to these rules, and one draw needn't show every extreme that they name: `list_place`: each number appears once.
All inputs are finite; a program needn't handle non-finite values.
Results may differ from a plain program's by a relative error of at most 0.0055.
Values may be sent and summed in bfloat16 or wider, within the bound.
A program may use at most 128 MiB of HBM per device.

v0:
```python
import jax
import jax.numpy as jnp
from jax import lax
from jax.sharding import PartitionSpec as P

HD = 64


norm_eps = 1e-12
range_eps = 1e-05


def norm_rows(values, gain):
    center = jnp.mean(values, -1, keepdims=True)
    shifted = values - center
    spread = jnp.mean(shifted * shifted, -1, keepdims=True)
    return shifted * lax.rsqrt(spread + norm_eps) * gain


def body(
    states,
    lengths,
    attn_in,
    attn_out,
    attn_gain,
    ffn_up,
    ffn_down,
    ffn_gain,
    centroids,
    assignment,
    list_place,
):
    doc_count, seq_len, width = states.shape
    model_ways = lax.axis_size("mp")
    docs_here = doc_count // model_ways
    head_width = attn_in.shape[2]
    local_heads = head_width // HD
    flat_rows = states.reshape(doc_count * seq_len, width)
    projected = jnp.einsum(
        "rd,sdc->src", flat_rows, attn_in, preferred_element_type=jnp.float32
    ).astype(jnp.bfloat16)
    shaped = projected.reshape(3, doc_count, seq_len, local_heads, HD)
    scores = jnp.einsum(
        "bqhc,bkhc->bhqk", shaped[0], shaped[1], preferred_element_type=jnp.float32
    ) * HD ** (-0.5)
    key_valid = jnp.arange(seq_len, dtype=jnp.int32)[None, :] < lengths[:, None]
    scores = jnp.where(key_valid[:, None, None, :], scores, -1e30)
    row_max = jnp.max(scores, -1, keepdims=True)
    exp_scores = jnp.exp(scores - row_max)
    attn_probs = (exp_scores / jnp.sum(exp_scores, -1, keepdims=True)).astype(jnp.bfloat16)
    context = jnp.einsum(
        "bhqk,bkhc->bqhc", attn_probs, shaped[2], preferred_element_type=jnp.float32
    ).astype(jnp.bfloat16)
    context = context.reshape(doc_count * seq_len, head_width)
    attn_part = jnp.dot(context, attn_out, preferred_element_type=jnp.float32)
    attn_total = lax.psum(attn_part.astype(jnp.bfloat16), "mp").astype(jnp.float32)
    hidden = norm_rows(flat_rows.astype(jnp.float32) + attn_total, attn_gain).astype(jnp.bfloat16)
    inner_act = jax.nn.gelu(
        jnp.dot(hidden, ffn_up, preferred_element_type=jnp.float32), approximate=False
    ).astype(jnp.bfloat16)
    position = lax.axis_index("mp")
    length_float = lengths.astype(jnp.float32)
    ffn_total = lax.psum(
        jnp.dot(inner_act, ffn_down, preferred_element_type=jnp.float32).astype(jnp.bfloat16), "mp"
    ).astype(jnp.float32)
    normed = norm_rows(hidden.astype(jnp.float32) + ffn_total, ffn_gain).reshape(
        doc_count, seq_len, width
    )
    pooled_all = jnp.sum(jnp.where(key_valid[:, :, None], normed, 0.0), 1) / length_float[:, None]
    pooled = lax.dynamic_slice_in_dim(pooled_all, position * docs_here, docs_here, 0)
    owned = centroids.shape[0]
    first_slot = lax.axis_index(("dp", "mp")) * owned
    local_slot = jnp.take(list_place, assignment) - first_slot
    slot_ids = jnp.arange(owned, dtype=jnp.int32)
    picker = (local_slot[:, None] == slot_ids[None, :]).astype(jnp.bfloat16)
    nearest = lax.psum_scatter(
        jnp.dot(picker, centroids, preferred_element_type=jnp.float32),
        ("dp", "mp"),
        scatter_dimension=0,
        tiled=True,
    )
    residual = pooled - nearest
    upper, negated = lax.pmax((jnp.max(residual, 0), jnp.max(-residual, 0)), ("dp", "mp"))
    lower = -negated
    codes = (residual - lower) / (upper - lower + range_eps)
    return (codes, lower, upper)


def solution(mesh):
    placed = (
        P("dp", None, None),
        P("dp"),
        P(None, None, "mp"),
        P("mp", None),
        P(),
        P(None, "mp"),
        P("mp", None),
        P(),
        P(("dp", "mp"), None),
        P(),
        P(),
    )
    return jax.shard_map(
        body,
        mesh=mesh,
        in_specs=placed,
        out_specs=(P(("dp", "mp"), None), P(), P()),
        check_vma=False,
    )
```

profile of v0, /device:TPU:0, one launch (start us, length us, event | category | flops | bytes accessed | tf_op | source)
XLA Modules:
  0.0 497.4 jit_solution(16501802587538947932)
XLA Ops:
  7.2 6.3 %fusion.25 = bf16[3,2048,256]{1,2,0:T(8,128)(2,1)S(1)} fusion(bf16[3,1024,256]{2,1,0:T(8,128)(2,1)} %param.13, bf16[2048,1024,1]{1,0,2:T(8,128)(2,1)} %bitcast.35), kind=kOutput, calls=%fused_computation.44 | convolution fusion | flops 3222798336 | bytes 8912896 | tf_op jit(solution)/shard_map/rd,sdc->src/dot_general | solution.py:39
  13.5 1.6 fusion.78
  15.1 2.6 squeeze.10
  17.7 2.7 squeeze.11
  20.5 1.6 squeeze.9
  22.0 11.7 %fusion.79 = (f32[4,4,512]{2,1,0:T(4,128)S(1)}, f32[4,4,512,512]{2,3,1,0:T(8,128)}) fusion(pred[4,512]{1,0:T(4,128)(4,1)S(1)} %iota_compare_fusion.2, bf16[4,512,4,64]{1,0,3,2:T(4,128)(2,1)} %squeeze.11, bf16[4,512,4,64]{1,0,3,2:T(4,128)(2,1)} %squeeze.10), kind=kOutput, calls=%fused_computation.103 | convolution fusion | flops 553648640 | bytes 18909184 | tf_op jit(solution)/shard_map/sub | solution.py:49
  33.8 7.3 %fusion.29 = bf16[4,512,4,64]{1,3,2,0:T(8,128)(2,1)S(1)} fusion(f32[4,4,512,512]{2,3,1,0:T(8,128)} %get-tuple-element.13, f32[4,4,512]{2,1,0:T(4,128)S(1)} %get-tuple-element.12, bf16[4,512,4,64]{1,0,3,2:T(4,128)(2,1)S(1)} %copy-done.6), kind=kOutput, calls=%fused_computation.47 | convolution fusion | flops 545783808 | bytes 18907136 | tf_op jit(solution)/shard_map/bhqk,bkhc->bqhc/dot_general | solution.py:51
  42.2 3.3 convolution_convert_fusion
  45.7 95.1 %all-reduce.6.cloned.1.call-done = bf16[2048,1024]{1,0:T(8,128)(2,1)} async-done(((bf16[2048,1024]{1,0:T(8,128)(2,1)}), bf16[2048,1024]{1,0:T(8,128)(2,1)}) %all-reduce.6.cloned.1.call-update) | async-done | bytes 4194320 | tf_op jit(solution)/shard_map/psum | solution.py:56
  140.8 4.8 fusion.17
  145.6 1.1 copy-done.4
  146.7 2.1 multiply_reduce_fusion.1
  148.9 3.5 multiply_convert_fusion
  152.4 28.4 %fusion.22 = bf16[2048,1024]{1,0:T(8,128)(2,1)} fusion(bf16[1024,1024]{1,0:T(8,128)(2,1)S(1)} %copy-done, bf16[2048,1024]{1,0:T(8,128)(2,1)} %multiply_convert_fusion, bf16[1024,1024]{1,0:T(8,128)(2,1)} %param.16), kind=kOutput, calls=%fused_computation.42 | convolution fusion | flops 8728346624 | bytes 12582912 | tf_op jit(solution)/shard_map/dot_general | solution.py:64
  181.0 1.4 gather_fusion
  182.4 1.2 fusion.42
  184.2 89.4 %all-reduce.8.cloned.1.call-done = bf16[2048,1024]{1,0:T(8,128)(2,1)} async-done(((bf16[2048,1024]{1,0:T(8,128)(2,1)}), bf16[2048,1024]{1,0:T(8,128)(2,1)}) %all-reduce.8.cloned.1.call-update) | async-done | bytes 4194320 | tf_op jit(solution)/shard_map/psum | solution.py:63
  273.6 4.8 fusion.19
  278.4 1.1 copy-done.3
  279.6 1.8 multiply_reduce_fusion
  281.4 2.6 select_reduce_fusion
  284.0 140.2 %all-reduce.10.cloned.1.call-done = f32[128,1024]{1,0:T(8,128)} async-done(((f32[128,1024]{1,0:T(8,128)}), f32[128,1024]{1,0:T(8,128)}) %all-reduce.10.cloned.1.call-update) | async-done | bytes 524304
  424.2 1.4 fusion.77
  425.6 64.7 %all-reduce.1 = (f32[1024]{0:T(1024)S(1)}, f32[1024]{0:T(1024)S(1)}) all-reduce(f32[1024]{0:T(1024)S(1)} %bitcast.38, f32[1024]{0:T(1024)S(1)} %bitcast.39), channel_id=1, replica_groups=mesh['dp'=32,'mp'=4] {'dp','mp'}, use_global_device_ids=true, to_apply=%region_11.12 | all-reduce | flops 2048 | bytes 16384 | tf_op jit(solution)/shard_map/pmax | solution.py:83
  (48 shorter events, 2.8 us)
Async XLA Ops:
  7.2 145.2 %copy-start = (bf16[1024,1024]{1,0:T(8,128)(2,1)S(1)}, bf16[1024,1024]{1,0:T(8,128)(2,1)}, u32[]{:S(2)}) copy-start(bf16[1024,1024]{1,0:T(8,128)(2,1)} %param.17) | copy-start | bytes 6291460
  7.2 133.6 %all-reduce.6.cloned.1.call-start = ((), (), s32[]{:S(2)}) async-start(), calls=%async_computation | async-start | bytes 8388608 | tf_op jit(solution)/shard_map/psum | solution.py:56
  13.5 6.9 %copy-start.13 = (s32[4]{0:T(128)S(1)}, s32[4]{0:T(128)}, u32[]{:S(2)}) copy-start(s32[4]{0:T(128)} %param.12) | copy-start | bytes 52
  22.0 11.7 %copy-start.6 = (bf16[4,512,4,64]{1,0,3,2:T(4,128)(2,1)S(1)}, bf16[4,512,4,64]{1,0,3,2:T(4,128)(2,1)}, u32[]{:S(2)}) copy-start(bf16[4,512,4,64]{1,0,3,2:T(4,128)(2,1)} %squeeze.9) | copy-start | bytes 3145732
  33.8 8.4 %copy-start.8 = (bf16[256,1024]{1,0:T(8,128)(2,1)S(1)}, bf16[256,1024]{1,0:T(8,128)(2,1)}, u32[]{:S(2)}) copy-start(bf16[256,1024]{1,0:T(8,128)(2,1)} %param.14) | copy-start | bytes 1572868
  45.5 103.4 %copy-start.10 = (f32[1024]{0:T(1024)S(1)}, f32[1024]{0:T(1024)}, u32[]{:S(2)}) copy-start(f32[1024]{0:T(1024)} %param.15) | copy-start | bytes 12292
  45.5 228.1 %all-reduce.8.cloned.1.call-start = ((), (), s32[]{:S(2)}) async-start(), calls=%async_computation.1 | async-start | bytes 8388608 | tf_op jit(solution)/shard_map/psum | solution.py:63
  140.8 4.8 copy-start.2
  140.8 5.9 %copy-start.4 = (bf16[2048,1024]{1,0:T(8,128)(2,1)S(1)}, bf16[2048,1024]{1,0:T(8,128)(2,1)}, u32[]{:S(2)}) copy-start(bf16[2048,1024]{1,0:T(8,128)(2,1)} %all-reduce.6.cloned.1.call-done) | copy-start | bytes 12582916
  152.4 28.5 %copy-start.14 = (s32[128]{0:T(128)S(1)}, s32[128]{0:T(128)}, u32[]{:S(2)}) copy-start(s32[128]{0:T(128)} %param.20) | copy-start | bytes 1540
  152.4 28.6 %copy-start.7 = (s32[65536]{0:T(1024)S(1)}, s32[65536]{0:T(1024)}, u32[]{:S(2)}) copy-start(s32[65536]{0:T(1024)} %param.21) | copy-start | bytes 786436
  152.4 30.0 %copy-start.5 = (bf16[512,1024]{1,0:T(8,128)(2,1)S(1)}, bf16[512,1024]{1,0:T(8,128)(2,1)}, u32[]{:S(2)}) copy-start(bf16[512,1024]{1,0:T(8,128)(2,1)} %param.19) | copy-start | bytes 3145732
  180.9 243.3 %all-reduce.10.cloned.1.call-start = ((), (), s32[]{:S(2)}) async-start(), calls=%async_computation.2 | async-start | bytes 1048576
  184.2 97.2 %copy-start.11 = (f32[1024]{0:T(1024)S(1)}, f32[1024]{0:T(1024)}, u32[]{:S(2)}) copy-start(f32[1024]{0:T(1024)} %param.18) | copy-start | bytes 12292
  273.6 4.8 copy-start.1
  273.6 5.9 %copy-start.3 = (bf16[2048,1024]{1,0:T(8,128)(2,1)S(1)}, bf16[2048,1024]{1,0:T(8,128)(2,1)}, u32[]{:S(2)}) copy-start(bf16[2048,1024]{1,0:T(8,128)(2,1)} %all-reduce.8.cloned.1.call-done) | copy-start | bytes 12582916
  490.3 0.6 copy-start.12
  490.3 0.6 copy-start.9
Sparse Core Ops, SparseCore 0:
  45.6 95.1 all-reduce.5
  181.0 92.5 all-reduce.7
  278.4 145.7 all-reduce.9
where the time goes:
time: 498 us; the launch traced here: 497 us
  waiting for transfers between devices  325 us (65%)
  blocking collectives  64.7 us (13%)
  matrix products  58.2 us (12%)
  other arithmetic  21.7 us (4%)
  between operations  14 us (3%)
  local copies, waits for them, and re-layouts  13.8 us (3%)
    unnamed x4, waiting for transfers between devices  140 us
    psum x1, waiting for transfers between devices, body(): lax.psum(attn_part.astype(jnp.bfloat16), 'mp').astype(jnp.float32)  95.1 us
    psum x1, waiting for transfers between devices, body(): lax.psum(jnp.dot(inner_act, ffn_down, preferred_element_type=jnp.float32)...  89.4 us
    pmax x1, blocking collectives, body(): lax.pmax((jnp.max(residual, 0), jnp.max(-residual, 0)), ('dp', 'mp'))  64.7 us
    dot_general x1, matrix products, body(): jnp.dot(inner_act, ffn_down, preferred_element_type=jnp.float32)  28.4 us
    sub x1, matrix products, body(): exp_scores = jnp.exp(scores - row_max)  11.7 us
  transfers between devices with their start and end apart: 3, of which 3 were waited for; matrix products, arithmetic and copies ran while one was open for 2% of the time, Pallas kernels for 0%

commit v1 on v0

v1 whole, which is shorter than its diff:
```python
import jax
import jax.numpy as jnp
from jax import lax
from jax.experimental import pallas as pl
from jax.experimental.pallas import tpu as pltpu
from jax.sharding import PartitionSpec as P

MESH = pl.DeviceIdType.MESH
SEQ, WIDTH, GROUP = 512, 1024, 256
CUTS = 4
CHUNKS = 1 + 2 * CUTS
UNITS = WIDTH // CUTS
NORM_EPS, RANGE_EPS = 1e-12, 1e-05
COMM = True

STEPS = {}


def at(tau, kind, k):
    STEPS.setdefault(tau, []).append((kind, k))


for _k in range(CHUNKS):
    _b = (7 * _k) // 2
    at(max(0, _b), "x1", _k)
    at(_b + 2, "x2", _k)
    at(_b + 4, "a1", _k)
    at(_b + 7, "a2", _k)
    at(_b + 10, "co", _k)
for _t, _n in ((6, "n0"), (10, "n1"), (13, "n2"), (15, "n3"), (18, "n4")):
    at(_t, _n, 0)

DOC_SLOTS = 5
DOC_STEPS = 4 * DOC_SLOTS


def norm_rows(values, gain):
    center = jnp.mean(values, -1, keepdims=True)
    shifted = values - center
    spread = jnp.mean(shifted * shifted, -1, keepdims=True)
    return shifted * lax.rsqrt(spread + NORM_EPS) * gain


def gelu(v):
    return 0.5 * v * (1.0 + lax.erf(v * 0.7071067811865476))


def mm(a, b):
    return jnp.dot(a, b, preferred_element_type=jnp.float32)


def kernel(
    lens,
    states,
    w_in,
    w_out,
    gain1,
    w_up,
    w_down,
    gain2,
    cents,
    asg,
    places,
    codes_o,
    lower_o,
    upper_o,
    st,
    win,
    wout,
    up,
    down,
    cen,
    qs,
    ks,
    vs,
    cs,
    cr,
    hid,
    acc,
    nb0,
    nz,
    ny0,
    ny,
    nc0,
    nc,
    nx0,
    nx,
    es,
    er,
    lsem,
    wsem,
    ssem,
    rsem,
    asem,
    psem,
    s2sem,
    csem,
    nsem,
    esem,
):
    dp = lax.axis_index("dp")
    x = lax.axis_index("mp")
    c = lax.rem(dp, 2)
    y = lax.rem(dp // 2, 4)
    z = dp // 8

    def dev(x_, y_, z_, c_):
        return ((z_ * 4 + y_) * 2 + c_, x_)

    def plus(v, d):
        return lax.rem(v + (d + 4), 4)

    def peer(axis, d):
        if axis == "x":
            return dev(plus(x, d), y, z, c)
        if axis == "y":
            return dev(x, plus(y, d), z, c)
        if axis == "z":
            return dev(x, y, plus(z, d), c)
        return dev(x, y, z, 1 - c)

    def remote(src, dst, send, recv, to):
        return pltpu.make_async_remote_copy(
            src_ref=src, dst_ref=dst, send_sem=send, recv_sem=recv, device_id=to, device_id_type=MESH
        )

    def load_doc(i):
        return pltpu.make_async_copy(states.at[plus(x, i + 1)], st.at[i], lsem.at[i])

    load_win = pltpu.make_async_copy(w_in, win, lsem.at[4])
    load_wout = pltpu.make_async_copy(w_out, wout.at[0], lsem.at[5])
    load_up = [
        pltpu.make_async_copy(
            w_up.at[:, pl.ds(j * UNITS, UNITS)], up.at[0, j], lsem.at[8 + j]
        )
        for j in range(CUTS)
    ]
    load_down = [
        pltpu.make_async_copy(
            w_down.at[pl.ds(j * UNITS, UNITS), :], down.at[0, j], lsem.at[8 + CUTS + j]
        )
        for j in range(CUTS)
    ]
    load_cen = pltpu.make_async_copy(cents, cen, lsem.at[6])
    load_doc(0).start()
    load_win.start()
    for i in range(1, 4):
        load_doc(i).start()

    def chunk(k):
        if k == 0:
            return wout, (), w_out, 0, 0, 16, WIDTH
        j = (k - 1) // 2
        if k % 2:
            return up, (j,), w_up, 0, j * UNITS, 64, UNITS
        return down, (j,), w_down, j * UNITS, 0, 16, WIDTH

    def rows(k, cc, color, q, n=1):
        size = chunk(k)[5]
        start = cc * (8 * size) + color * (4 * size) + q * size
        return pl.ds(pl.multiple_of(start, size), n * size)

    def place(k, r, rws, cols=slice(None)):
        buf, mid = chunk(k)[:2]
        return buf.at[(r,) + mid + (rws, cols)]

    def mine(color):
        return y if color == 0 else z

    def step_x1(k, color, d):
        _, _, src, row0, col0, size, ncols = chunk(k)
        start = row0 + c * (8 * size) + color * (4 * size) + mine(color) * size
        piece = src.at[pl.ds(pl.multiple_of(start, size), size), pl.ds(col0, ncols)]
        dst = place(k, 3 if d > 0 else 1, rows(k, c, color, mine(color)))
        n = color * 2 + (0 if d > 0 else 1)
        return remote(piece, dst, wsem.at[k, n], ssem.at[k, n], peer("x", d))

    def step_x2(k, color):
        d = 1 if color == 0 else -1
        rws = rows(k, c, color, mine(color))
        return remote(
            place(k, 3 if d > 0 else 1, rws),
            place(k, 2, rws),
            wsem.at[k, 4 + color],
            ssem.at[k, 4 + color],
            peer("x", d),
        )

    def step_a1(k, color, d, arriving=False):
        q = plus(mine(color), -d) if arriving else mine(color)
        part = place(k, pl.ds(1, 3), rows(k, c, color, q))
        n = color * 4 + (0 if d > 0 else 1)
        return remote(
            part, part, asem.at[k, n], rsem.at[k, n], peer("yz"[color], d)
        )

    def step_a2(k, color, d, arriving=False):
        q = plus(mine(color), -2 * d if arriving else -d)
        size, ncols = chunk(k)[5:]
        half = 0 if d > 0 else 1
        if size >= 32:
            start = c * (8 * size) + color * (4 * size) + q * size + half * (size // 2)
            part = place(k, pl.ds(1, 3), pl.ds(pl.multiple_of(start, size // 2), size // 2))
        else:
            part = place(
                k, pl.ds(1, 3), rows(k, c, color, q), pl.ds(half * (ncols // 2), ncols // 2)
            )
        n = color * 4 + 2 + half
        return remote(
            part, part, asem.at[k, n], rsem.at[k, n], peer("yz"[color], d)
        )

    def step_co(k, color, arriving=False):
        part = place(k, pl.ds(1, 3), rows(k, 1 - c if arriving else c, color, 0, 4))
        return remote(part, part, s2sem.at[k, color], psem.at[k, color], peer("c", 1))

    both = [(color, d) for color in range(2) for d in (1, -1)]

    def near_z(d):
        rws = pl.ds(pl.multiple_of(plus(z, d) * 32, 32), 32)
        return remote(nb0.at[rws, :], nz.at[d - 1], nsem.at[0, 0, d - 1], nsem.at[1, 0, d - 1], peer("z", d))

    def near_y(d):
        rws = pl.ds(pl.multiple_of(plus(y, d) * 8, 8), 8)
        return remote(ny0.at[rws, :], ny.at[d - 1], nsem.at[0, 1, d - 1], nsem.at[1, 1, d - 1], peer("y", d))

    def near_c():
        return remote(nc0, nc, nsem.at[0, 2, 0], nsem.at[1, 2, 0], peer("c", 1))

    def near_x(d):
        return remote(nx0, nx.at[d - 1], nsem.at[0, 3, d - 1], nsem.at[1, 3, d - 1], peer("x", d))

    def near_first():
        load_cen.wait()
        ids = asg[...]
        hi = ids // 128
        lo = ids - hi * 128
        pick_hi = (hi == lax.broadcasted_iota(jnp.int32, (128, 512), 1)).astype(jnp.float32).astype(jnp.bfloat16)
        table = places[...]
        high = table // 256
        low = table - high * 256
        found = (
            mm(pick_hi, high.astype(jnp.float32).astype(jnp.bfloat16)) * 256.0
            + mm(pick_hi, low.astype(jnp.float32).astype(jnp.bfloat16))
        )
        lane = lax.broadcasted_iota(jnp.int32, (128, 128), 1)
        slot = jnp.sum(jnp.where(lane == lo, found, 0.0), -1, keepdims=True)
        first = ((dp * 4 + x) * 512).astype(jnp.float32)
        own = lax.broadcasted_iota(jnp.int32, (128, 512), 1).astype(jnp.float32)
        picker = (slot - first == own).astype(jnp.float32).astype(jnp.bfloat16)
        nb0[...] = mm(picker, cen[...]).astype(jnp.bfloat16)

    def event(kind, k):
        if kind == "x1":
            for color, d in both:
                step_x1(k, color, d).start()
        elif kind == "x2":
            step_x1(k, 0, 1).wait_recv()
            step_x2(k, 0).start()
            step_x1(k, 1, -1).wait_recv()
            step_x2(k, 1).start()
        elif kind == "a1":
            step_x1(k, 0, -1).wait_recv()
            step_x1(k, 1, 1).wait_recv()
            for color in range(2):
                step_x2(k, color).wait_recv()
            for color, d in both:
                step_a1(k, color, d).start()
        elif kind == "a2":
            for color, d in both:
                step_a1(k, color, d, True).wait_recv()
                step_a2(k, color, d).start()
        elif kind == "co":
            for color, d in both:
                step_a2(k, color, d, True).wait_recv()
            for color in range(2):
                step_co(k, color).start()
        elif kind == "n0":
            near_first()
            for d in (1, 2, 3):
                near_z(d).start()
        elif kind == "n1":
            total = nb0[pl.ds(pl.multiple_of(z * 32, 32), 32), :].astype(jnp.float32)
            for d in (1, 2, 3):
                near_z(d).wait_recv()
                total += nz[d - 1].astype(jnp.float32)
            ny0[...] = total
            for d in (1, 2, 3):
                near_y(d).start()
        elif kind == "n2":
            total = ny0[pl.ds(pl.multiple_of(y * 8, 8), 8), :]
            for d in (1, 2, 3):
                near_y(d).wait_recv()
                total += ny[d - 1]
            nc0[...] = total
            near_c().start()
        elif kind == "n3":
            near_c().wait_recv()
            nx0[...] = nc0[...] + nc[...]
            for d in (1, 2, 3):
                near_x(d).start()

    def flush(tau):
        if COMM:
            for kind, k in STEPS.get(tau, []):
                event(kind, k)

    def in_loop(i, slot):
        for ii in range(4):
            if STEPS.get(ii * DOC_SLOTS + slot):

                @pl.when(i == ii)
                def _():
                    flush(ii * DOC_SLOTS + slot)

    def send_ctx(i):
        return remote(cs.at[i], cr.at[3 - i], csem.at[0, i], csem.at[1, i], peer("x", i + 1))

    if COMM:
        barrier = pltpu.get_barrier_semaphore()
        peers = [peer(a, d) for a in "xyz" for d in (1, 2, 3)] + [peer("c", 1)]
        for p in peers:
            pl.semaphore_signal(barrier, inc=1, device_id=p, device_id_type=MESH)
        pl.semaphore_wait(barrier, len(peers))

    lane = lax.broadcasted_iota(jnp.int32, (256, 128), 1) < 64
    lane_all = lax.broadcasted_iota(jnp.int32, (SEQ, 128), 1) < 64

    def late_loads():
        load_cen.start()
        load_wout.start()
        for j in range(CUTS):
            load_up[j].start()
            load_down[j].start()

    @pl.loop(0, 4)
    def _(i):
        in_loop(i, 0)

        @pl.when(i == 0)
        def _():
            load_win.wait()
            late_loads()

        load_doc(i).wait()
        doc = st[i]
        q32 = mm(doc, win[0]) * 0.125
        for p in range(2):
            part = q32[:, p * 128 : p * 128 + 128]
            qs[2 * p] = jnp.where(lane_all, part, 0.0).astype(jnp.bfloat16)
            qs[2 * p + 1] = jnp.where(lane_all, 0.0, part).astype(jnp.bfloat16)
        ks[...] = mm(doc, win[1]).astype(jnp.bfloat16)
        v32 = mm(doc, win[2])
        for p in range(2):
            part = v32[:, p * 128 : p * 128 + 128]
            vs[2 * p] = jnp.where(lane_all, part, 1.0).astype(jnp.bfloat16)
            vs[2 * p + 1] = jnp.where(lane_all, 1.0, part).astype(jnp.bfloat16)
        bias = jnp.where(
            lax.broadcasted_iota(jnp.int32, (1, SEQ), 1) < lens[plus(x, i + 1)], 0.0, -1e30
        )
        for unit in range(4):
            p, qb = unit // 2, unit % 2
            in_loop(i, unit + 1)
            outs = []
            keys = ks[:, p * 128 : p * 128 + 128]
            for h in range(2):
                scores = lax.dot_general(
                    qs[2 * p + h, qb * 256 : qb * 256 + 256],
                    keys,
                    (((1,), (1,)), ((), ())),
                    preferred_element_type=jnp.float32,
                )
                scores = scores + bias
                e = jnp.exp(scores - jnp.max(scores, -1, keepdims=True)).astype(jnp.bfloat16)
                outs.append(mm(e, vs[2 * p + h]))
            top = jnp.where(lane, outs[0], outs[1])
            mass = pltpu.roll(jnp.where(lane, outs[1], outs[0]), 64, 1)
            cs[i, qb * 256 : qb * 256 + 256, p * 128 : p * 128 + 128] = (top / mass).astype(jnp.bfloat16)
        if COMM:
            for ii in range(3):

                @pl.when(i == ii)
                def _():
                    send_ctx(ii).start()

    tau = DOC_STEPS
    flush(tau)
    load_wout.wait()
    acc[...] = st[3].astype(jnp.float32) + mm(cs[3], wout[0])
    tau += 1
    flush(tau)
    if COMM:
        for color in range(2):
            step_co(0, color, True).wait_recv()
        for i in range(3):
            send_ctx(i).wait_recv()
    part = mm(cr[1], wout[1]) + mm(cr[2], wout[2]) + mm(cr[3], wout[3])
    hidden = norm_rows(acc[...] + part, gain1[...])
    hid[...] = hidden.astype(jnp.bfloat16)
    acc[...] = hid[...].astype(jnp.float32)

    def ffn(rs, js):
        for mb in range(2):
            rws = pl.ds(mb * 256, 256)
            h = hid[rws, :]
            total = acc[rws, :]
            for r in rs:
                for j in js:
                    act = gelu(mm(h, up[r, j])).astype(jnp.bfloat16)
                    total += mm(act, down[r, j])
            acc[rws, :] = total

    for jj in range(2):
        tau += 1
        flush(tau)
        for j in (2 * jj, 2 * jj + 1):
            load_up[j].wait()
            load_down[j].wait()
        ffn((0,), (2 * jj, 2 * jj + 1))
    last = max(STEPS)

    def arrive(j):
        for k in (1 + 2 * j, 2 + 2 * j):
            for color in range(2):
                step_co(k, color, True).wait_recv()

    for j in range(CUTS):
        need = max(t for t, ev in STEPS.items() if ("co", 2 + 2 * j) in ev)
        for _ in range(3):
            tau += 1
            flush(tau)
        while tau < need:
            tau += 1
            flush(tau)
        if COMM:
            arrive(j)
        ffn((1, 2, 3), (j,))
    assert tau >= last

    normed = norm_rows(acc[...], gain2[...])
    own_len = lens[x]
    live = lax.broadcasted_iota(jnp.int32, (SEQ, 1), 0) < own_len
    pooled = jnp.sum(jnp.where(live, normed, 0.0), 0, keepdims=True) / own_len.astype(jnp.float32)
    near = nx0[...]
    if COMM:
        for d in (1, 2, 3):
            near_x(d).wait_recv()
            near += nx[d - 1]
    mark = lax.broadcasted_iota(jnp.int32, (8, 1), 0) == c * 4 + x
    near = jnp.sum(jnp.where(mark, near, 0.0), 0, keepdims=True)
    flat = pooled - near
    for j in range(8):
        es[0, 0, j : j + 1, :] = flat[:, j * 128 : j * 128 + 128]
    residual = es[0, 0]
    es[0, 1] = -residual

    def extreme(stage, d):
        return remote(
            es.at[stage], er.at[stage, d - 1], esem.at[0, stage, d - 1], esem.at[1, stage, d - 1],
            peer("cxyz"[stage], d),
        )

    def reach(stage):
        return (1,) if stage == 0 else (1, 2, 3)

    best = jnp.concatenate([es[0, 0][None], es[0, 1][None]], 0)
    if COMM:
        for stage in range(4):
            if stage:
                es[stage] = best
            for d in reach(stage):
                extreme(stage, d).start()
            for d in reach(stage):
                extreme(stage, d).wait_recv()
                best = jnp.maximum(best, er[stage, d - 1])
    upper = best[0]
    lower = -best[1]
    upper_o[...] = upper
    lower_o[...] = lower
    codes_o[...] = (residual - lower) / (upper - lower + RANGE_EPS)

    if COMM:
        for k in range(CHUNKS):
            for color, d in both:
                step_x1(k, color, d).wait_send()
                step_a1(k, color, d).wait_send()
                step_a2(k, color, d).wait_send()
            for color in range(2):
                step_x2(k, color).wait_send()
                step_co(k, color).wait_send()
        for d in (1, 2, 3):
            near_z(d).wait_send()
            near_y(d).wait_send()
            near_x(d).wait_send()
        near_c().wait_send()
        for i in range(3):
            send_ctx(i).wait_send()
        for stage in range(4):
            for d in reach(stage):
                extreme(stage, d).wait_send()
    else:
        load_cen.wait()


def body(
    states,
    lengths,
    attn_in,
    attn_out,
    attn_gain,
    ffn_up,
    ffn_down,
    ffn_gain,
    centroids,
    assignment,
    list_place,
):
    hbm = pl.BlockSpec(memory_space=pl.ANY)
    vmem = pl.BlockSpec(memory_space=pltpu.VMEM)
    smem = pl.BlockSpec(memory_space=pltpu.SMEM)
    bf, f32 = jnp.bfloat16, jnp.float32
    tile = jax.ShapeDtypeStruct((8, 128), f32)
    dma = pltpu.SemaphoreType.DMA
    codes, lower, upper = pl.pallas_call(
        kernel,
        out_shape=(tile, tile, tile),
        in_specs=[smem, hbm, hbm, hbm, vmem, hbm, hbm, vmem, hbm, vmem, vmem],
        out_specs=(vmem, vmem, vmem),
        scratch_shapes=[
            pltpu.VMEM((4, SEQ, WIDTH), bf),
            pltpu.VMEM((3, WIDTH, GROUP), bf),
            pltpu.VMEM((4, GROUP, WIDTH), bf),
            pltpu.VMEM((4, CUTS, WIDTH, UNITS), bf),
            pltpu.VMEM((4, CUTS, UNITS, WIDTH), bf),
            pltpu.VMEM((512, WIDTH), bf),
            pltpu.VMEM((4, SEQ, 128), bf),
            pltpu.VMEM((SEQ, GROUP), bf),
            pltpu.VMEM((4, SEQ, 128), bf),
            pltpu.VMEM((4, SEQ, GROUP), bf),
            pltpu.VMEM((4, SEQ, GROUP), bf),
            pltpu.VMEM((SEQ, WIDTH), bf),
            pltpu.VMEM((SEQ, WIDTH), f32),
            pltpu.VMEM((128, WIDTH), bf),
            pltpu.VMEM((3, 32, WIDTH), bf),
            pltpu.VMEM((32, WIDTH), f32),
            pltpu.VMEM((3, 8, WIDTH), f32),
            pltpu.VMEM((8, WIDTH), f32),
            pltpu.VMEM((8, WIDTH), f32),
            pltpu.VMEM((8, WIDTH), f32),
            pltpu.VMEM((3, 8, WIDTH), f32),
            pltpu.VMEM((4, 2, 8, 128), f32),
            pltpu.VMEM((4, 3, 2, 8, 128), f32),
            dma((8 + 2 * CUTS,)),
            dma((CHUNKS, 6)),
            dma((CHUNKS, 6)),
            dma((CHUNKS, 8)),
            dma((CHUNKS, 8)),
            dma((CHUNKS, 2)),
            dma((CHUNKS, 2)),
            dma((2, 3)),
            dma((2, 4, 3)),
            dma((2, 4, 3)),
        ],
        compiler_params=pltpu.CompilerParams(
            vmem_limit_bytes=60 * 2**20,
            **(dict(collective_id=0, has_side_effects=True) if COMM else {}),
        ),
        name="encode",
    )(
        lengths,
        states,
        attn_in,
        attn_out,
        attn_gain.reshape(1, WIDTH),
        ffn_up,
        ffn_down,
        ffn_gain.reshape(1, WIDTH),
        centroids,
        assignment.reshape(128, 1),
        list_place.reshape(512, 128),
    )
    return codes.reshape(1, WIDTH), lower.reshape(WIDTH), upper.reshape(WIDTH)


def solution(mesh):
    placed = (
        P("dp", None, None),
        P("dp"),
        P(None, None, "mp"),
        P("mp", None),
        P(),
        P(None, "mp"),
        P("mp", None),
        P(),
        P(("dp", "mp"), None),
        P(),
        P(),
    )
    return jax.shard_map(
        body,
        mesh=mesh,
        in_specs=placed,
        out_specs=(P(("dp", "mp"), None), P(), P()),
        check_vma=False,
    )
```

time: 498 us -> 109 us (0.22)
  waiting for transfers between devices: 325 us -> 0 us
  Pallas kernels: 0 us -> 103 us
  blocking collectives: 64.7 us -> 0 us
  matrix products: 58.2 us -> 0 us
  other arithmetic: 21.7 us -> 0 us
  between operations: 14 us -> 0.64 us
  local copies, waits for them, and re-layouts: 13.8 us -> 5.2 us
    psum x2 -> x0, waiting for transfers between devices: 185 us -> none  [the longest x1 95.1 us: body(): lax.psum(attn_part.astype(jnp.bfloat16), 'mp').astype(jnp.float32)]
    unnamed x4 -> x0, waiting for transfers between devices: 140 us -> none
    pallas_call x0 -> x1, Pallas kernels: none -> 103 us  [body(): pl.pallas_call(kernel, out_shape=(tile, tile, tile), in_specs=[smem, hbm,...]
    pmax x1 -> x0, blocking collectives: 64.7 us -> none  [body(): lax.pmax((jnp.max(residual, 0), jnp.max(-residual, 0)), ('dp', 'mp'))]
    dot_general x5 -> x0, matrix products: 46.4 us -> none  [the longest x1 28.4 us: body(): jnp.dot(inner_act, ffn_down, preferred_element_type=jnp.float32)]
    reduce_sum x5 -> x0, other arithmetic: 16.1 us -> none  [the longest x2 9.51 us: norm_rows(): center = jnp.mean(values, -1, keepdims=True)]
    sub x1 -> x0, matrix products: 11.7 us -> none  [body(): exp_scores = jnp.exp(scores - row_max)]
    squeeze x3 -> x0, local copies, waits for them, and re-layouts: 6.88 us -> none  [the longest x1 2.65 us: body(): shaped[1]]
  transfers between devices with their start and end apart: 3 -> 0, of which waited for: 3 -> 0; matrix products, arithmetic and copies ran while one was open for 2% -> 0% of each run, Pallas kernels for 0% -> 0%
where the time goes in v1:
time: 109 us
  Pallas kernels  103 us (94%)
  local copies, waits for them, and re-layouts  5.2 us (5%)
    pallas_call x1, Pallas kernels, body(): pl.pallas_call(kernel, out_shape=(tile, tile, tile), in_specs=[smem, hbm,...  103 us
    unnamed x3, local copies, waits for them, and re-layouts  3.82 us

profile of v1, /device:TPU:0, one launch (start us, length us, event | category | flops | bytes accessed | tf_op | source)
XLA Modules:
  0.0 108.6 jit_solution(9631512687257577723)
XLA Ops:
  0.6 1.4 %copy.14.asg = s32[128,1]{1,0:T(8,128)} copy(s32[128,1]{0,1:T(1,128)} %bitcast.13) | data formatting | bytes 1024 | tf_op jit(solution)/shard_map/reshape | solution.py:579
  2.0 102.8 %encode.1 = (f32[8,128]{1,0:T(8,128)}, f32[8,128]{1,0:T(8,128)}, f32[8,128]{1,0:T(8,128)}) custom-call(s32[4]{0:T(128)} %lens.1, bf16[4,512,1024]{2,1,0:T(8,128)(2,1)} %states.1, bf16[3,1024,256]{2,1,0:T(8,128)(2,1)} %w_in.1, bf16[256,1024]{1,0:T(8,128)(2,1)} %w_out.1, f32[1,1024]{1,0:T(1,128)} %bitcast.8, bf16[1024,1024]{1,0:T(8,128)(2,1)} %w_up.1, ...), custom_call_target="tpu_custom_call" | custom-call | tf_op jit(solution)/shard_map/encode/pallas_call | solution.py:524
  104.8 1.3 %copy.18 = f32[1,1024]{1,0:T(1,128)} copy(f32[1,1024]{1,0:T(1,128)} %bitcast.12) | data formatting | bytes 8192
  106.1 1.3 %copy.19 = f32[1024]{0:T(1024)} copy(f32[1024]{0:T(1024)} %bitcast.11) | data formatting | bytes 8192
  107.3 1.3 %copy.20 = f32[1024]{0:T(1024)} copy(f32[1024]{0:T(1024)} %bitcast.10) | data formatting | bytes 8192

commit v2 on v1

v2 whole, which is shorter than its diff:
```python
import jax
import jax.numpy as jnp
from jax import lax
from jax.experimental import pallas as pl
from jax.experimental.pallas import tpu as pltpu
from jax.sharding import PartitionSpec as P

MESH = pl.DeviceIdType.MESH
SEQ, WIDTH, GROUP = 512, 1024, 256
CUTS = 4
QB = 1
CHUNKS = 1 + 2 * CUTS
UNITS = WIDTH // CUTS
NORM_EPS, RANGE_EPS = 1e-12, 1e-05
COMM = True

DOC_ORDER = (2, 1, 3, 0)
CTX_SLOT = (3, 2, 1)

STEPS = {
    "u00": (("x1", 0, 0), ("x1", 1, 0), ("x1", 2, 0), ("n0", 0, 0),),
    "u01": (("x1", 3, 0), ("x1", 4, 0), ("x1", 5, 0),),
    "q1": (("a1", 0, 0),),
    "u10": (("x2", 0, 0), ("x1", 6, 0), ("x1", 7, 0), ("x1", 8, 0),),
    "u11": (("a1", 1, 0), ("a1", 2, 0), ("n1", 0, 0), ("x2", 1, 0), ("x2", 2, 0),),
    "q2": (("a2", 0, 0),),
    "u21": (("a2", 1, 0), ("a1", 3, 0), ("a1", 4, 0), ("x2", 4, 0),),
    "q3": (("a2", 2, 0), ("a1", 5, 0), ("x2", 5, 0), ("x2", 3, 0),),
    "u30": (("co", 0, 0), ("co", 1, 0), ("n2", 0, 0),),
    "u31": (("a1", 0, 1), ("a2", 3, 0),),
    "o0": (("a2", 4, 0), ("a1", 6, 0), ("a1", 7, 0), ("co", 2, 0), ("x2", 6, 0), ("x2", 7, 0),),
    "o1": (("a2", 5, 0), ("a1", 8, 0), ("n3", 0, 0), ("a2", 0, 1), ("co", 3, 0), ("co", 4, 0), ("a1", 1, 1), ("a2", 6, 0), ("a1", 2, 1), ("x2", 8, 0), ("a2", 7, 0), ("co", 5, 0), ("a2", 8, 0), ("a1", 4, 1), ("co", 0, 1), ("a1", 5, 1), ("a2", 1, 1), ("a1", 3, 1), ("co", 6, 0), ("a1", 6, 1),),
    "f00": (("a2", 2, 1), ("a1", 7, 1), ("co", 7, 0), ("co", 8, 0),),
    "f01": (("a2", 4, 1), ("a2", 5, 1), ("a1", 8, 1),),
    "f10": (("a2", 3, 1), ("co", 1, 1),),
    "f11": (("a2", 6, 1),),
    "g00": (("co", 2, 1),),
    "g01": (("a2", 7, 1),),
    "g10": (("co", 4, 1), ("co", 5, 1),),
    "g11": (("a2", 8, 1), ("co", 3, 1),),
    "g20": (("co", 6, 1),),
    "g30": (("co", 7, 1),),
    "h00": (("co", 8, 1),),
}
STEPS_OF = {ev: n for n, ev in enumerate(e for evs in STEPS.values() for e in evs)}


def norm_rows(values, gain):
    center = jnp.mean(values, -1, keepdims=True)
    shifted = values - center
    spread = jnp.mean(shifted * shifted, -1, keepdims=True)
    return shifted * lax.rsqrt(spread + NORM_EPS) * gain


def gelu(v):
    return 0.5 * v * (1.0 + lax.erf(v * 0.7071067811865476))


def mm(a, b):
    return jnp.dot(a, b, preferred_element_type=jnp.float32)


def mm_rows(a, b):
    return lax.dot_general(a, b, (((0,), (0,)), ((), ())), preferred_element_type=jnp.float32)


def kernel(
    lens,
    states,
    w_in,
    w_out,
    gain1,
    w_up,
    w_down,
    gain2,
    cents,
    asg,
    places,
    res_o,
    ext_o,
    st,
    win,
    wout,
    up,
    down,
    cen,
    qs,
    ks,
    vs,
    cs,
    cr,
    hid,
    acc,
    nb0,
    nz,
    ny0,
    ny,
    nc0,
    nc,
    nx0,
    nx,
    es,
    er,
    lsem,
    wsem,
    ssem,
    rsem,
    asem,
    psem,
    s2sem,
    csem,
    nsem,
    esem,
):
    dp = lax.axis_index("dp")
    x = lax.axis_index("mp")
    c = lax.rem(dp, 2)
    y = lax.rem(dp // 2, 4)
    z = dp // 8

    def dev(x_, y_, z_, c_):
        return ((z_ * 4 + y_) * 2 + c_, x_)

    def plus(v, d):
        return lax.rem(v + (d + 4), 4)

    def peer(axis, d):
        if axis == "x":
            return dev(plus(x, d), y, z, c)
        if axis == "y":
            return dev(x, plus(y, d), z, c)
        if axis == "z":
            return dev(x, y, plus(z, d), c)
        return dev(x, y, z, 1 - c)

    def group(stage, n):
        if stage == 0:
            return dev(plus(x, n // 2), y, z, lax.rem(c + n, 2))
        return peer("xyz"[stage], n)

    def remote(src, dst, send, recv, to):
        return pltpu.make_async_remote_copy(
            src_ref=src, dst_ref=dst, send_sem=send, recv_sem=recv, device_id=to, device_id_type=MESH
        )

    def turn(i):
        return lax.rem(x + (2 + 3 * i + 3 * (i // 2) + 2 * (i // 3)), 4)

    def load_doc(i):
        return pltpu.make_async_copy(states.at[turn(i)], st.at[i], lsem.at[i])

    load_win = pltpu.make_async_copy(w_in, win, lsem.at[4])
    load_wout = pltpu.make_async_copy(w_out, wout.at[0], lsem.at[5])
    load_up = [
        pltpu.make_async_copy(
            w_up.at[:, pl.ds(j * UNITS, UNITS)], up.at[0, j], lsem.at[8 + j]
        )
        for j in range(CUTS)
    ]
    load_down = [
        pltpu.make_async_copy(
            w_down.at[pl.ds(j * UNITS, UNITS), :], down.at[0, j], lsem.at[8 + CUTS + j]
        )
        for j in range(CUTS)
    ]
    load_cen = pltpu.make_async_copy(cents, cen, lsem.at[6])
    load_doc(0).start()
    load_win.start()
    load_cen.start()
    for i in range(1, 4):
        load_doc(i).start()
    load_wout.start()
    for j in range(CUTS):
        load_up[j].start()
        load_down[j].start()

    def chunk(k):
        if k == 0:
            return wout, (), w_out, 0, 0, 16, WIDTH
        j = (k - 1) // 2
        if k % 2:
            return up, (j,), w_up, 0, j * UNITS, 64, UNITS
        return down, (j,), w_down, j * UNITS, 0, 16, WIDTH

    def rows(k, cc, color, q, n=1):
        size = chunk(k)[5]
        start = cc * (8 * size) + color * (4 * size) + q * size
        return pl.ds(pl.multiple_of(start, size), n * size)

    def place(k, r, rws, cols=slice(None)):
        buf, mid = chunk(k)[:2]
        return buf.at[(r,) + mid + (rws, cols)]

    def mine(color):
        return y if color == 0 else z

    def step_x1(k, color, d):
        _, _, src, row0, col0, size, ncols = chunk(k)
        start = row0 + c * (8 * size) + color * (4 * size) + mine(color) * size
        piece = src.at[pl.ds(pl.multiple_of(start, size), size), pl.ds(col0, ncols)]
        dst = place(k, 2 if d > 0 else 1, rows(k, c, color, mine(color)))
        n = color * 2 + (0 if d > 0 else 1)
        return remote(piece, dst, wsem.at[k, n], ssem.at[k, n], peer("x", d))

    def step_x2(k, color):
        d = 1 if color == 0 else -1
        rws = rows(k, c, color, mine(color))
        return remote(
            place(k, 2 if d > 0 else 1, rws),
            place(k, 3, rws),
            wsem.at[k, 4 + color],
            ssem.at[k, 4 + color],
            peer("x", d),
        )

    def span(p):
        return pl.ds(1, 2) if p == 0 else pl.ds(3, 1)

    def step_a1(k, p, color, d, arriving=False):
        q = plus(mine(color), -d) if arriving else mine(color)
        part = place(k, span(p), rows(k, c, color, q))
        n = color * 4 + (0 if d > 0 else 1)
        return remote(
            part, part, asem.at[k, p, n], rsem.at[k, p, n], peer("yz"[color], d)
        )

    def step_a2(k, p, color, d, arriving=False):
        q = plus(mine(color), -2 * d if arriving else -d)
        size, ncols = chunk(k)[5:]
        half = 0 if d > 0 else 1
        if size >= 32:
            start = c * (8 * size) + color * (4 * size) + q * size + half * (size // 2)
            part = place(k, span(p), pl.ds(pl.multiple_of(start, size // 2), size // 2))
        else:
            part = place(
                k, span(p), rows(k, c, color, q), pl.ds(half * (ncols // 2), ncols // 2)
            )
        n = color * 4 + 2 + half
        return remote(
            part, part, asem.at[k, p, n], rsem.at[k, p, n], peer("yz"[color], d)
        )

    def step_co(k, p, color, arriving=False):
        part = place(k, span(p), rows(k, 1 - c if arriving else c, color, 0, 4))
        return remote(part, part, s2sem.at[k, p, color], psem.at[k, p, color], peer("c", 1))

    both = [(color, d) for color in range(2) for d in (1, -1)]

    def near_z(d):
        rws = pl.ds(pl.multiple_of(plus(z, d) * 32, 32), 32)
        return remote(nb0.at[rws, :], nz.at[d - 1], nsem.at[0, 0, d - 1], nsem.at[1, 0, d - 1], peer("z", d))

    def near_y(d):
        rws = pl.ds(pl.multiple_of(plus(y, d) * 8, 8), 8)
        return remote(ny0.at[rws, :], ny.at[d - 1], nsem.at[0, 1, d - 1], nsem.at[1, 1, d - 1], peer("y", d))

    def near_c():
        return remote(nc0, nc, nsem.at[0, 2, 0], nsem.at[1, 2, 0], peer("c", 1))

    def near_x(d):
        return remote(nx0, nx.at[d - 1], nsem.at[0, 3, d - 1], nsem.at[1, 3, d - 1], peer("x", d))

    def near_first():
        load_cen.wait()
        ids = asg[...]
        hi = ids // 128
        lo = ids - hi * 128
        slots = lax.broadcasted_iota(jnp.int32, (512, 128), 0)
        pick_hi = (hi == slots).astype(jnp.float32).astype(jnp.bfloat16)
        table = places[...]
        high = table // 256
        low = table - high * 256
        found = (
            mm_rows(high.astype(jnp.float32).astype(jnp.bfloat16), pick_hi) * 256.0
            + mm_rows(low.astype(jnp.float32).astype(jnp.bfloat16), pick_hi)
        )
        lanes = lax.broadcasted_iota(jnp.int32, (128, 128), 0)
        slot = jnp.sum(jnp.where(lanes == lo, found, 0.0), 0, keepdims=True)
        first = ((dp * 4 + x) * 512).astype(jnp.float32)
        picker = (slot - first == slots.astype(jnp.float32)).astype(jnp.float32).astype(jnp.bfloat16)
        nb0[...] = mm_rows(picker, cen[...]).astype(jnp.bfloat16)

    def event(kind, k, p):
        if kind == "x1":
            for color, d in both:
                step_x1(k, color, d).start()
        elif kind == "x2":
            before = STEPS_OF[("x2", k, 0)] < STEPS_OF[("a1", k, 0)]
            for color, d in ((0, 1), (1, -1)):
                if before:
                    step_x1(k, color, d).wait_recv()
                step_x2(k, color).start()
        elif kind == "a1":
            if p == 0:
                step_x1(k, 0, -1).wait_recv()
                step_x1(k, 1, 1).wait_recv()
                if STEPS_OF[("x2", k, 0)] > STEPS_OF[("a1", k, 0)]:
                    step_x1(k, 0, 1).wait_recv()
                    step_x1(k, 1, -1).wait_recv()
            else:
                for color in range(2):
                    step_x2(k, color).wait_recv()
            for color, d in both:
                step_a1(k, p, color, d).start()
        elif kind == "a2":
            for color, d in both:
                step_a1(k, p, color, d, True).wait_recv()
                step_a2(k, p, color, d).start()
        elif kind == "co":
            for color, d in both:
                step_a2(k, p, color, d, True).wait_recv()
            for color in range(2):
                step_co(k, p, color).start()
        elif kind == "n0":
            for d in (1, 2, 3):
                near_z(d).start()
        elif kind == "n1":
            total = nb0[pl.ds(pl.multiple_of(z * 32, 32), 32), :].astype(jnp.float32)
            for d in (1, 2, 3):
                near_z(d).wait_recv()
                total += nz[d - 1].astype(jnp.float32)
            ny0[...] = total
            for d in (1, 2, 3):
                near_y(d).start()
        elif kind == "n2":
            total = ny0[pl.ds(pl.multiple_of(y * 8, 8), 8), :]
            for d in (1, 2, 3):
                near_y(d).wait_recv()
                total += ny[d - 1]
            nc0[...] = total
            near_c().start()
        elif kind == "n3":
            near_c().wait_recv()
            nx0[...] = nc0[...] + nc[...]
            for d in (1, 2, 3):
                near_x(d).start()

    def flush(tau):
        if COMM:
            for kind, k, p in STEPS.get(tau, ()):
                event(kind, k, p)

    def in_loop(i, slot):
        for ii in range(4):
            tau = f"q{ii + 1}" if slot == 2 else f"u{ii}{slot}"
            if STEPS.get(tau):

                @pl.when(i == ii)
                def _():
                    flush(tau)

    def send_ctx(i, p):
        cols = pl.ds(p * 128, 128)
        return remote(
            cs.at[i, :, cols],
            cr.at[CTX_SLOT[i], :, cols],
            csem.at[0, i, p],
            csem.at[1, i, p],
            peer("x", DOC_ORDER[i]),
        )

    if COMM:
        barrier = pltpu.get_barrier_semaphore()
        peers = [group(0, n) for n in range(1, 8)] + [peer(a, d) for a in "yz" for d in (1, 2, 3)]
        for p in peers:
            pl.semaphore_signal(barrier, inc=1, device_id=p, device_id_type=MESH)

    lane = lax.broadcasted_iota(jnp.int32, (SEQ // QB, 128), 1) < 64
    lane_all = lax.broadcasted_iota(jnp.int32, (SEQ, 128), 1) < 64

    def project(i):
        load_doc(i).wait()
        doc = st[i]
        q32 = mm(doc, win[0]) * 0.125
        for p in range(2):
            part = q32[:, p * 128 : p * 128 + 128]
            qs[2 * p] = jnp.where(lane_all, part, 0.0).astype(jnp.bfloat16)
            qs[2 * p + 1] = jnp.where(lane_all, 0.0, part).astype(jnp.bfloat16)
        ks[...] = mm(doc, win[1]).astype(jnp.bfloat16)
        v32 = mm(doc, win[2])
        for p in range(2):
            part = v32[:, p * 128 : p * 128 + 128]
            vs[2 * p] = jnp.where(lane_all, part, 1.0).astype(jnp.bfloat16)
            vs[2 * p + 1] = jnp.where(lane_all, 1.0, part).astype(jnp.bfloat16)
    load_win.wait()
    project(0)
    if COMM:
        near_first()
        pl.semaphore_wait(barrier, len(peers))

    @pl.loop(0, 4)
    def _(i):
        bias = jnp.where(
            lax.broadcasted_iota(jnp.int32, (1, SEQ), 1) < lens[turn(i)], 0.0, -1e30
        )
        for p in range(2):
            in_loop(i, p)
            keys = ks[:, p * 128 : p * 128 + 128]
            for qb in range(QB):
                outs = []
                rws = pl.ds(qb * (SEQ // QB), SEQ // QB)
                for h in range(2):
                    scores = lax.dot_general(
                        qs[2 * p + h, rws],
                        keys,
                        (((1,), (1,)), ((), ())),
                        preferred_element_type=jnp.float32,
                    )
                    scores = scores + bias
                    e = jnp.exp(scores - jnp.max(scores, -1, keepdims=True)).astype(jnp.bfloat16)
                    outs.append(mm(e, vs[2 * p + h]))
                top = jnp.where(lane, outs[0], outs[1])
                mass = pltpu.roll(jnp.where(lane, outs[1], outs[0]), 64, 1)
                cs[i, rws, p * 128 : p * 128 + 128] = (top / mass).astype(jnp.bfloat16)
            if COMM:
                for ii in range(3):

                    @pl.when(i == ii)
                    def _():
                        send_ctx(ii, p).start()

        in_loop(i, 2)

        @pl.when(i < 3)
        def _():
            project(i + 1)

    def arrive(k, p):
        if COMM:
            for color in range(2):
                step_co(k, p, color, True).wait_recv()

    flush("o0")
    load_wout.wait()
    acc[...] = st[3].astype(jnp.float32) + mm(cs[3], wout[0])
    flush("o1")
    arrive(0, 0)
    arrive(0, 1)
    if COMM:
        for i in range(3):
            for p in range(2):
                send_ctx(i, p).wait_recv()
    part = mm(cr[1], wout[1]) + mm(cr[2], wout[2]) + mm(cr[3], wout[3])
    hidden = norm_rows(acc[...] + part, gain1[...])
    hid[...] = hidden.astype(jnp.bfloat16)
    acc[...] = hid[...].astype(jnp.float32)

    def ffn(parts, between):
        for mb in range(2):
            if mb:
                flush(between)
            rws = pl.ds(mb * 256, 256)
            h = hid[rws, :]
            total = acc[rws, :]
            for r, j in parts:
                act = gelu(mm(h, up[r, j])).astype(jnp.bfloat16)
                total += mm(act, down[r, j])
            acc[rws, :] = total

    for n in range(CUTS // 2):
        flush(f"f{n}0")
        for j in (2 * n, 2 * n + 1):
            load_up[j].wait()
            load_down[j].wait()
        ffn(((0, 2 * n), (0, 2 * n + 1)), f"f{n}1")
    for j in range(CUTS):
        flush(f"g{j}0")
        arrive(1 + 2 * j, 0)
        arrive(2 + 2 * j, 0)
        ffn(((1, j), (2, j)), f"g{j}1")
    for n in range(CUTS // 2):
        flush(f"h{n}0")
        for k in range(1 + 4 * n, 5 + 4 * n):
            arrive(k, 1)
        ffn(((3, 2 * n), (3, 2 * n + 1)), f"h{n}1")
    flush("end")

    normed = norm_rows(acc[...], gain2[...])
    own_len = lens[x]
    live = lax.broadcasted_iota(jnp.int32, (SEQ, 1), 0) < own_len
    pooled = jnp.sum(jnp.where(live, normed, 0.0), 0, keepdims=True) / own_len.astype(jnp.float32)
    near = nx0[...]
    if COMM:
        for d in (1, 2, 3):
            near_x(d).wait_recv()
            near += nx[d - 1]
    mark = lax.broadcasted_iota(jnp.int32, (8, 1), 0) == c * 4 + x
    near = jnp.sum(jnp.where(mark, near, 0.0), 0, keepdims=True)
    flat = pooled - near
    for j in range(8):
        es[0, 0, j : j + 1, :] = flat[:, j * 128 : j * 128 + 128]
    residual = es[0, 0]
    es[0, 1] = -residual

    def extreme(stage, n):
        return remote(
            es.at[stage], er.at[stage, n - 1], esem.at[0, stage, n - 1], esem.at[1, stage, n - 1],
            group(stage, n),
        )

    def reach(stage):
        return range(1, 8 if stage == 0 else 4)

    def sent(k):
        for color, d in both:
            step_x1(k, color, d).wait_send()
            for p in range(2):
                step_a1(k, p, color, d).wait_send()
                step_a2(k, p, color, d).wait_send()
        for color in range(2):
            step_x2(k, color).wait_send()
            for p in range(2):
                step_co(k, p, color).wait_send()

    best = jnp.concatenate([es[0, 0][None], es[0, 1][None]], 0)
    if COMM:
        for stage in range(3):
            if stage:
                es[stage] = best
            for d in reach(stage):
                extreme(stage, d).start()
            for k in range(3 * stage, 3 * stage + 3):
                sent(k)
            for d in reach(stage):
                extreme(stage, d).wait_recv()
                best = jnp.maximum(best, er[stage, d - 1])
    res_o[...] = residual
    ext_o[...] = best

    if COMM:
        for d in (1, 2, 3):
            near_z(d).wait_send()
            near_y(d).wait_send()
            near_x(d).wait_send()
        near_c().wait_send()
        for i in range(3):
            for p in range(2):
                send_ctx(i, p).wait_send()
        for stage in range(3):
            for d in reach(stage):
                extreme(stage, d).wait_send()
    else:
        load_cen.wait()


def finish(res, ext, codes_o, lower_o, upper_o):
    upper = ext[0]
    lower = -ext[1]
    upper_o[...] = upper
    lower_o[...] = lower
    codes_o[...] = (res[...] - lower) / (upper - lower + RANGE_EPS)


def body(
    states,
    lengths,
    attn_in,
    attn_out,
    attn_gain,
    ffn_up,
    ffn_down,
    ffn_gain,
    centroids,
    assignment,
    list_place,
):
    hbm = pl.BlockSpec(memory_space=pl.ANY)
    vmem = pl.BlockSpec(memory_space=pltpu.VMEM)
    smem = pl.BlockSpec(memory_space=pltpu.SMEM)
    bf, f32 = jnp.bfloat16, jnp.float32
    tile = jax.ShapeDtypeStruct((8, 128), f32)
    dma = pltpu.SemaphoreType.DMA
    residual, extremes = pl.pallas_call(
        kernel,
        out_shape=(tile, jax.ShapeDtypeStruct((2, 8, 128), f32)),
        in_specs=[smem, hbm, hbm, hbm, vmem, hbm, hbm, vmem, hbm, vmem, vmem],
        out_specs=(vmem, vmem),
        scratch_shapes=[
            pltpu.VMEM((4, SEQ, WIDTH), bf),
            pltpu.VMEM((3, WIDTH, GROUP), bf),
            pltpu.VMEM((4, GROUP, WIDTH), bf),
            pltpu.VMEM((4, CUTS, WIDTH, UNITS), bf),
            pltpu.VMEM((4, CUTS, UNITS, WIDTH), bf),
            pltpu.VMEM((512, WIDTH), bf),
            pltpu.VMEM((4, SEQ, 128), bf),
            pltpu.VMEM((SEQ, GROUP), bf),
            pltpu.VMEM((4, SEQ, 128), bf),
            pltpu.VMEM((4, SEQ, GROUP), bf),
            pltpu.VMEM((4, SEQ, GROUP), bf),
            pltpu.VMEM((SEQ, WIDTH), bf),
            pltpu.VMEM((SEQ, WIDTH), f32),
            pltpu.VMEM((128, WIDTH), bf),
            pltpu.VMEM((3, 32, WIDTH), bf),
            pltpu.VMEM((32, WIDTH), f32),
            pltpu.VMEM((3, 8, WIDTH), f32),
            pltpu.VMEM((8, WIDTH), f32),
            pltpu.VMEM((8, WIDTH), f32),
            pltpu.VMEM((8, WIDTH), f32),
            pltpu.VMEM((3, 8, WIDTH), f32),
            pltpu.VMEM((3, 2, 8, 128), f32),
            pltpu.VMEM((3, 7, 2, 8, 128), f32),
            dma((8 + 2 * CUTS,)),
            dma((CHUNKS, 6)),
            dma((CHUNKS, 6)),
            dma((CHUNKS, 2, 8)),
            dma((CHUNKS, 2, 8)),
            dma((CHUNKS, 2, 2)),
            dma((CHUNKS, 2, 2)),
            dma((2, 3, 2)),
            dma((2, 4, 3)),
            dma((2, 3, 7)),
        ],
        compiler_params=pltpu.CompilerParams(
            vmem_limit_bytes=60 * 2**20,
            **(dict(collective_id=0, has_side_effects=True) if COMM else {}),
        ),
        name="encode",
    )(
        lengths,
        states,
        attn_in,
        attn_out,
        attn_gain.reshape(1, WIDTH),
        ffn_up,
        ffn_down,
        ffn_gain.reshape(1, WIDTH),
        centroids,
        assignment.reshape(1, 128),
        list_place.reshape(512, 128),
    )
    codes, lower, upper = pl.pallas_call(
        finish,
        out_shape=(tile, tile, tile),
        in_specs=[vmem, vmem],
        out_specs=(vmem, vmem, vmem),
        name="finish",
    )(residual, extremes)
    return codes.reshape(1, WIDTH), lower.reshape(WIDTH), upper.reshape(WIDTH)


def solution(mesh):
    placed = (
        P("dp", None, None),
        P("dp"),
        P(None, None, "mp"),
        P("mp", None),
        P(),
        P(None, "mp"),
        P("mp", None),
        P(),
        P(("dp", "mp"), None),
        P(),
        P(),
    )
    return jax.shard_map(
        body,
        mesh=mesh,
        in_specs=placed,
        out_specs=(P(("dp", "mp"), None), P(), P()),
        check_vma=False,
    )
```

time: 109 us -> 77.6 us (0.71)
  Pallas kernels: 103 us -> 76.8 us
  local copies, waits for them, and re-layouts: 5.2 us -> 0 us
    pallas_call x1 -> x2, Pallas kernels: 103 us -> 76.8 us  [the longest x1 75.5 us: body(): pl.pallas_call(kernel, out_shape=(tile, jax.ShapeDtypeStruct((2, 8, 128),...]
    unnamed x3 -> x0, local copies, waits for them, and re-layouts: 3.82 us -> none
    reshape x1 -> x0, local copies, waits for them, and re-layouts: 1.38 us -> none  [body(): assignment.reshape(128, 1)]
where the time goes in v2:
time: 77.6 us; the launch traced here: 77.4 us
  Pallas kernels  76.8 us (99%)
    pallas_call x1, Pallas kernels, body(): pl.pallas_call(kernel, out_shape=(tile, jax.ShapeDtypeStruct((2, 8, 128),...  75.5 us

profile of v2, /device:TPU:0, one launch (start us, length us, event | category | flops | bytes accessed | tf_op | source)
XLA Modules:
  0.0 77.4 jit_solution(123524001565263307)
XLA Ops:
  0.6 75.5 %encode.1 = (f32[8,128]{1,0:T(8,128)}, f32[2,8,128]{2,1,0:T(8,128)}) custom-call(s32[4]{0:T(128)} %lens.1, bf16[4,512,1024]{2,1,0:T(8,128)(2,1)} %states.1, bf16[3,1024,256]{2,1,0:T(8,128)(2,1)} %w_in.1, bf16[256,1024]{1,0:T(8,128)(2,1)} %w_out.1, f32[1,1024]{1,0:T(1,128)} %bitcast.8, bf16[1024,1024]{1,0:T(8,128)(2,1)} %w_up.1, bf16[1024,1024]{1,0:T(8,128)(2,1)} %w_down.1, ...), custom_call_target="tpu_custom_call" | custom-call | tf_op jit(solution)/shard_map/encode/pallas_call | solution.py:573
  76.1 1.3 %finish.1 = (f32[8,128]{1,0:T(8,128)}, f32[8,128]{1,0:T(8,128)}, f32[8,128]{1,0:T(8,128)}) custom-call(f32[8,128]{1,0:T(8,128)} %get-tuple-element.8.res, f32[2,8,128]{2,1,0:T(8,128)} %get-tuple-element.9.ext), custom_call_target="tpu_custom_call" | custom-call | tf_op jit(solution)/shard_map/finish/pallas_call | solution.py:631

commit v3 on v2

--- a/solution.py
+++ b/solution.py
@@ -18,29 +18,29 @@
 CTX_SLOT = (3, 2, 1)
 
 STEPS = {
-    "u00": (("x1", 0, 0), ("x1", 1, 0), ("x1", 2, 0), ("n0", 0, 0),),
-    "u01": (("x1", 3, 0), ("x1", 4, 0), ("x1", 5, 0),),
-    "q1": (("a1", 0, 0),),
-    "u10": (("x2", 0, 0), ("x1", 6, 0), ("x1", 7, 0), ("x1", 8, 0),),
-    "u11": (("a1", 1, 0), ("a1", 2, 0), ("n1", 0, 0), ("x2", 1, 0), ("x2", 2, 0),),
-    "q2": (("a2", 0, 0),),
-    "u21": (("a2", 1, 0), ("a1", 3, 0), ("a1", 4, 0), ("x2", 4, 0),),
-    "q3": (("a2", 2, 0), ("a1", 5, 0), ("x2", 5, 0), ("x2", 3, 0),),
-    "u30": (("co", 0, 0), ("co", 1, 0), ("n2", 0, 0),),
-    "u31": (("a1", 0, 1), ("a2", 3, 0),),
-    "o0": (("a2", 4, 0), ("a1", 6, 0), ("a1", 7, 0), ("co", 2, 0), ("x2", 6, 0), ("x2", 7, 0),),
-    "o1": (("a2", 5, 0), ("a1", 8, 0), ("n3", 0, 0), ("a2", 0, 1), ("co", 3, 0), ("co", 4, 0), ("a1", 1, 1), ("a2", 6, 0), ("a1", 2, 1), ("x2", 8, 0), ("a2", 7, 0), ("co", 5, 0), ("a2", 8, 0), ("a1", 4, 1), ("co", 0, 1), ("a1", 5, 1), ("a2", 1, 1), ("a1", 3, 1), ("co", 6, 0), ("a1", 6, 1),),
-    "f00": (("a2", 2, 1), ("a1", 7, 1), ("co", 7, 0), ("co", 8, 0),),
-    "f01": (("a2", 4, 1), ("a2", 5, 1), ("a1", 8, 1),),
-    "f10": (("a2", 3, 1), ("co", 1, 1),),
-    "f11": (("a2", 6, 1),),
-    "g00": (("co", 2, 1),),
-    "g01": (("a2", 7, 1),),
-    "g10": (("co", 4, 1), ("co", 5, 1),),
-    "g11": (("a2", 8, 1), ("co", 3, 1),),
-    "g20": (("co", 6, 1),),
-    "g30": (("co", 7, 1),),
-    "h00": (("co", 8, 1),),
+    "u00": (("x1", 0, 0), ("x1", 1, 0), ("x1", 2, 0), ("x1", 3, 0), ("x1", 4, 0), ("n0", 0, 0),),
+    "q1": (("a1", 0, 0), ("x2", 0, 0), ("x1", 5, 0), ("x1", 6, 0), ("x1", 7, 0),),
+    "u10": (("a1", 1, 0), ("a1", 2, 0), ("n1", 0, 0), ("x2", 2, 0),),
+    "u11": (("a1", 3, 0),),
+    "q2": (("a2", 0, 0), ("a1", 4, 0), ("x2", 4, 0), ("x2", 1, 0),),
+    "u20": (("a2", 1, 0), ("a2", 2, 0),),
+    "q3": (("a1", 0, 1), ("co", 0, 0), ("a2", 3, 0), ("n2", 0, 0), ("x1", 8, 0),),
+    "u30": (("a2", 4, 0), ("a1", 5, 0), ("x2", 5, 0),),
+    "u31": (("a2", 0, 1), ("a1", 6, 0), ("co", 1, 0), ("co", 2, 0), ("n3", 0, 0),),
+    "o0": (("a1", 7, 0), ("a1", 2, 1), ("co", 3, 0), ("co", 4, 0),),
+    "o1": (("co", 0, 1), ("a2", 5, 0), ("x2", 3, 0), ("x2", 7, 0), ("a2", 6, 0), ("a2", 7, 0), ("a1", 4, 1), ("a2", 2, 1),),
+    "f00": (("a1", 8, 0), ("a1", 1, 1), ("co", 5, 0), ("co", 6, 0), ("x2", 8, 0),),
+    "f01": (("a1", 5, 1), ("co", 7, 0), ("x2", 6, 0),),
+    "f10": (("a2", 4, 1), ("a1", 3, 1), ("co", 2, 1),),
+    "f11": (("a1", 7, 1),),
+    "g00": (("a2", 8, 0), ("a1", 8, 1),),
+    "g01": (("a2", 1, 1), ("a1", 6, 1),),
+    "g10": (("a2", 5, 1), ("co", 4, 1),),
+    "g11": (("a2", 3, 1),),
+    "g20": (("a2", 7, 1),),
+    "g21": (("co", 8, 0),),
+    "g30": (("a2", 8, 1), ("co", 1, 1), ("a2", 6, 1), ("co", 5, 1), ("co", 3, 1), ("co", 7, 1),),
+    "h00": (("co", 8, 1), ("co", 6, 1),),
 }
 STEPS_OF = {ev: n for n, ev in enumerate(e for evs in STEPS.values() for e in evs)}
 
@@ -124,7 +124,15 @@
     def plus(v, d):
         return lax.rem(v + (d + 4), 4)
 
+    near_by = {
+        (a, d): dev(*(plus(v, d) if n == a else v for n, v in (("x", x), ("y", y), ("z", z))), c)
+        for a in "xyz"
+        for d in (1, -1)
+    }
+
     def peer(axis, d):
+        if (axis, d) in near_by:
+            return near_by[axis, d]
         if axis == "x":
             return dev(plus(x, d), y, z, c)
         if axis == "y":
@@ -241,7 +249,7 @@
         )
 
     def step_co(k, p, color, arriving=False):
-        part = place(k, span(p), rows(k, 1 - c if arriving else c, color, 0, 4))
+        part = place(k, span(p), rows(k, 1 - c if arriving else c, 0, 0, 8))
         return remote(part, part, s2sem.at[k, p, color], psem.at[k, p, color], peer("c", 1))
 
     both = [(color, d) for color in range(2) for d in (1, -1)]
@@ -309,9 +317,9 @@
         elif kind == "co":
             for color, d in both:
                 step_a2(k, p, color, d, True).wait_recv()
-            for color in range(2):
-                step_co(k, p, color).start()
+            step_co(k, p, 0).start()
         elif kind == "n0":
+            near_first()
             for d in (1, 2, 3):
                 near_z(d).start()
         elif kind == "n1":
@@ -385,7 +393,6 @@
     load_win.wait()
     project(0)
     if COMM:
-        near_first()
         pl.semaphore_wait(barrier, len(peers))
 
     @pl.loop(0, 4)
@@ -427,8 +434,7 @@
 
     def arrive(k, p):
         if COMM:
-            for color in range(2):
-                step_co(k, p, color, True).wait_recv()
+            step_co(k, p, 0, True).wait_recv()
 
     flush("o0")
     load_wout.wait()
@@ -509,8 +515,8 @@
                 step_a2(k, p, color, d).wait_send()
         for color in range(2):
             step_x2(k, color).wait_send()
-            for p in range(2):
-                step_co(k, p, color).wait_send()
+        for p in range(2):
+            step_co(k, p, 0).wait_send()
 
     best = jnp.concatenate([es[0, 0][None], es[0, 1][None]], 0)
     if COMM:
@@ -604,8 +610,8 @@
             dma((CHUNKS, 6)),
             dma((CHUNKS, 2, 8)),
             dma((CHUNKS, 2, 8)),
-            dma((CHUNKS, 2, 2)),
-            dma((CHUNKS, 2, 2)),
+            dma((CHUNKS, 2, 1)),
+            dma((CHUNKS, 2, 1)),
             dma((2, 3, 2)),
             dma((2, 4, 3)),
             dma((2, 3, 7)),

time: 77.6 us -> 75.4 us (0.972)
  Pallas kernels: 76.8 us -> 74.6 us
    pallas_call x1, Pallas kernels: 75.5 us -> 73.3 us  [body(): pl.pallas_call(kernel, out_shape=(tile, jax.ShapeDtypeStruct((2, 8, 128),...]
where the time goes in v3:
time: 75.4 us; the launch traced here: 75.3 us
  Pallas kernels  74.6 us (99%)
    pallas_call x1, Pallas kernels, body(): pl.pallas_call(kernel, out_shape=(tile, jax.ShapeDtypeStruct((2, 8, 128),...  73.3 us

profile of v3, /device:TPU:0, one launch (start us, length us, event | category | flops | bytes accessed | tf_op | source)
XLA Modules:
  0.0 75.3 jit_solution(3763166863346088249)
XLA Ops:
  0.6 73.3 %encode.1 = (f32[8,128]{1,0:T(8,128)}, f32[2,8,128]{2,1,0:T(8,128)}) custom-call(s32[4]{0:T(128)} %lens.1, bf16[4,512,1024]{2,1,0:T(8,128)(2,1)} %states.1, bf16[3,1024,256]{2,1,0:T(8,128)(2,1)} %w_in.1, bf16[256,1024]{1,0:T(8,128)(2,1)} %w_out.1, f32[1,1024]{1,0:T(1,128)} %bitcast.8, bf16[1024,1024]{1,0:T(8,128)(2,1)} %w_up.1, bf16[1024,1024]{1,0:T(8,128)(2,1)} %w_down.1, ...), custom_call_target="tpu_custom_call" | custom-call | tf_op jit(solution)/shard_map/encode/pallas_call | solution.py:579
  74.0 1.3 %finish.1 = (f32[8,128]{1,0:T(8,128)}, f32[8,128]{1,0:T(8,128)}, f32[8,128]{1,0:T(8,128)}) custom-call(f32[8,128]{1,0:T(8,128)} %get-tuple-element.8.res, f32[2,8,128]{2,1,0:T(8,128)} %get-tuple-element.9.ext), custom_call_target="tpu_custom_call" | custom-call | tf_op jit(solution)/shard_map/finish/pallas_call | solution.py:637
